TPU v7x, 32 devices: a whole 2x2x4 slice. The times are simulated.
32 devices in a mesh: blade: 4 (over y, x), dp: 8 (over z, core).
Axes of the slice: x: 2, y: 2, z: 4, core: 2. Of those that a mesh axis runs over, the one named last changes fastest.
Arguments:
- inputs: bfloat16 [64, 4, 48, 4096], P('dp', 'blade'), may hold values from -6 to 6
- cotangent: bfloat16 [64, 4, 48, 4096], P('dp', 'blade'), may hold values from -6 to 6
- norm_table: float32 [16], replicated, may hold values from 0.5 to 2
- sample_index: int32 [64], P('dp'), may hold values from 0 to 15
- spec_weight: float32 [4, 256, 2, 48, 48], P('blade', 'dp'), may hold values from -0.875 to 0.875
- spec_first: float32 [4, 256, 2, 48, 48], P('blade', 'dp'), may hold values from -6 to 6
- spec_second: float32 [4, 256, 2, 48, 48], P('blade', 'dp'), may hold values from 0.32 to 1.344
- lin_weight: float32 [4, 48, 48], P('blade'), may hold values from -0.4375 to 0.4375
- lin_first: float32 [4, 48, 48], P('blade'), may hold values from -640 to 640
- lin_second: float32 [4, 48, 48], P('blade'), may hold values from 786.432 to 3145.728
Outputs:
- output: bfloat16 [64, 4, 48, 4096], P('dp', 'blade')
- input_grad: float32 [64, 4, 48, 4096], P('dp', 'blade')
- spec_new: float32 [4, 256, 2, 48, 48], P('blade', 'dp')
- spec_first_new: float32 [4, 256, 2, 48, 48], P('blade', 'dp')
- spec_second_new: float32 [4, 256, 2, 48, 48], P('blade', 'dp')
- lin_new: float32 [4, 48, 48], P('blade')
- lin_first_new: float32 [4, 48, 48], P('blade')
- lin_second_new: float32 [4, 48, 48], P('blade')
All inputs are finite; a program needn't handle non-finite values.
Results may differ from a plain program's by a relative error of at most 0.014.
Values may be sent and summed in bfloat16 or wider, within the bound.
No kernel may reach another device: no remote copies, remote signals or barrier semaphores. Data moves between devices by JAX's collectives and lax.ppermute only.
A program may use at most 192 MiB of HBM per device.

v0:
```python
from functools import partial
import math
import jax
import jax.numpy as jnp
from jax import lax
from jax.sharding import PartitionSpec as P

GRID = 64
MSIDE = 16
NTAB = 16
STEP_COUNT = 5
NPIX = 4096
MODES = 256
BETA_ONE = 0.9
BETA_TWO = 0.999
EPSILON = 1e-08
RATE = 0.1
DECAY = 0.01


def blade_sign(left_blade, right_blade):
    return 1 - 2 * (left_blade // 2 % 2) * (right_blade % 2)


def tables():
    pix_ids = jnp.arange(NPIX, dtype=jnp.int32)
    pix_row = pix_ids // GRID
    pix_col = pix_ids % GRID
    mode_ids = jnp.arange(MODES, dtype=jnp.int32)
    row_index = mode_ids // MSIDE
    col_freq = mode_ids % MSIDE
    row_freq = jnp.where(row_index < MSIDE // 2, row_index, GRID - MSIDE + row_index)
    phase_int = (pix_row[:, None] * row_freq[None, :] + pix_col[:, None] * col_freq[None, :]) % GRID
    angles = phase_int.astype(jnp.float32) * (2.0 * math.pi / GRID)
    forward = jnp.concatenate([jnp.cos(angles), -jnp.sin(angles)], axis=1) / GRID
    factor = jnp.where(col_freq == 0, 1.0, 2.0).astype(jnp.float32)
    factor = jnp.concatenate([factor, factor])
    return (forward.astype(jnp.bfloat16), (forward * factor[None, :]).astype(jnp.bfloat16))


def sign_matrix(own_blade, first_side):
    lane_ids = jnp.arange(4, dtype=jnp.int32)
    row_ids = lane_ids[:, None]
    col_ids = lane_ids[None, :]
    matches = jnp.bitwise_xor(row_ids, col_ids) == own_blade
    if first_side == "col":
        values = blade_sign(col_ids, own_blade)
    elif first_side == "row":
        values = blade_sign(row_ids, col_ids)
    else:
        values = blade_sign(own_blade, col_ids)
    return jnp.where(matches, values, 0).astype(jnp.bfloat16)


def adamw(weight, first, second, grad):
    first_new = BETA_ONE * first + (1.0 - BETA_ONE) * grad
    second_new = BETA_TWO * second + (1.0 - BETA_TWO) * grad * grad
    corr_one = 1.0 - BETA_ONE**STEP_COUNT
    corr_two = 1.0 - BETA_TWO**STEP_COUNT
    update = first_new / corr_one / (jnp.sqrt(second_new / corr_two) + EPSILON)
    return (weight - RATE * (update + DECAY * weight), first_new, second_new)


def body(
    inputs,
    cotangent,
    norm_table,
    sample_index,
    spec_weight,
    spec_first,
    spec_second,
    lin_weight,
    lin_first,
    lin_second,
):
    own_blade = lax.axis_index("blade")
    num_samples = inputs.shape[0]
    num_chans = inputs.shape[2]
    forward_table, inverse_table = tables()
    matches = sample_index[:, None] == jnp.arange(NTAB, dtype=jnp.int32)[None, :]
    normalizer = jnp.sum(jnp.where(matches, norm_table[None, :], 0.0), axis=1)[:, None, None, None]
    normed = inputs.astype(jnp.float32) / normalizer
    normed_low = normed.astype(jnp.bfloat16)
    lin_low = lin_weight.astype(jnp.bfloat16)
    spec_low = spec_weight.astype(jnp.bfloat16)
    own_modes = jnp.einsum(
        "sjcp,pn->sjcn", normed_low, forward_table, preferred_element_type=jnp.float32
    ).astype(jnp.bfloat16)
    normed_all, lin_all, modes_all = (
        lax.all_gather(normed_low, "blade", axis=1, tiled=True),
        lax.all_gather(lin_low, "blade", axis=0, tiled=True),
        lax.all_gather(own_modes, "blade", axis=1, tiled=True),
    )
    modes_real = modes_all[..., :MODES]
    modes_imag = modes_all[..., MODES:]
    block_in = lax.all_gather(spec_low, "dp", axis=1, tiled=True)
    w_real = block_in[0, :, 0]
    w_imag = block_in[0, :, 1]
    form = partial(jnp.einsum, "sjcm,mco->sjom", preferred_element_type=jnp.float32)
    out_real = form(modes_real, w_real) - form(modes_imag, w_imag)
    out_imag = form(modes_real, w_imag) + form(modes_imag, w_real)
    products = jnp.stack([out_real, out_imag], axis=3)
    blade_mix = sign_matrix(own_blade, "col")
    partial_spec = jnp.einsum("ij,sjcrm->sicrm", blade_mix.astype(jnp.float32), products)
    spec_sum = lax.psum_scatter(partial_spec, "blade", scatter_dimension=1, tiled=True)
    spec_out = spec_sum.reshape(num_samples, 1, num_chans, 2 * MODES).astype(jnp.bfloat16)
    spatial = jnp.einsum(
        "sjcn,pn->sjcp", spec_out, inverse_table, preferred_element_type=jnp.float32
    )
    forward_lin = sign_matrix(own_blade, "row")
    lin_cat = jnp.einsum(
        "jk,kco->jco", forward_lin, lin_all, preferred_element_type=jnp.float32
    ).astype(jnp.bfloat16)
    linear = jnp.einsum("sjcp,jco->sop", normed_all, lin_cat, preferred_element_type=jnp.float32)[
        :, None
    ]
    pre = spatial + linear
    activated, gelu_pullback = jax.vjp(partial(jax.nn.gelu, approximate=False), pre)
    output = (normed + activated).astype(jnp.bfloat16)
    cot_float = cotangent.astype(jnp.float32)
    grad_pre = gelu_pullback(cot_float)[0].astype(jnp.bfloat16)
    grad_spec = jnp.einsum(
        "sjcp,pn->sjcn", grad_pre, inverse_table, preferred_element_type=jnp.float32
    ).astype(jnp.bfloat16)
    pre_all, spec_grad_all = (
        lax.all_gather(grad_pre, "blade", axis=1, tiled=True),
        lax.all_gather(grad_spec, "blade", axis=1, tiled=True),
    )
    mixed_spec = jnp.einsum(
        "ij,sicn->sjcn", blade_mix, spec_grad_all, preferred_element_type=jnp.float32
    ).astype(jnp.bfloat16)
    mixed_pre = jnp.einsum(
        "ij,sicp->sjcp", blade_mix, pre_all, preferred_element_type=jnp.float32
    ).astype(jnp.bfloat16)
    grad_real = mixed_spec[..., :MODES]
    grad_imag = mixed_spec[..., MODES:]
    d_real = grad_real
    d_imag = grad_imag
    form = partial(jnp.einsum, "sjcm,sjom->mco", preferred_element_type=jnp.float32)
    term_real = form(modes_real, d_real) + form(modes_imag, d_imag)
    term_imag = form(modes_real, d_imag) - form(modes_imag, d_real)
    spec_grad = lax.psum_scatter(
        jnp.stack([term_real, term_imag], axis=1).astype(jnp.bfloat16),
        "dp",
        scatter_dimension=0,
        tiled=True,
    ).astype(jnp.float32)[None]
    block_in = lax.all_gather(spec_low, "dp", axis=1, tiled=True)
    d_real = grad_real
    d_imag = grad_imag
    w_real = block_in[0, :, 0]
    w_imag = block_in[0, :, 1]
    form = partial(jnp.einsum, "sjom,mco->sjcm", preferred_element_type=jnp.float32)
    back_real = form(d_real, w_real) + form(d_imag, w_imag)
    back_imag = form(d_imag, w_real) - form(d_real, w_imag)
    back_all = jnp.stack([back_real, back_imag], axis=3)
    grad_modes = lax.psum_scatter(
        back_all.astype(jnp.bfloat16), "blade", scatter_dimension=1, tiled=True
    ).astype(jnp.float32)
    grad_modes = grad_modes.reshape(num_samples, 1, num_chans, 2 * MODES).astype(jnp.bfloat16)
    from_spec = jnp.einsum(
        "sjcn,pn->sjcp", grad_modes, forward_table, preferred_element_type=jnp.float32
    )
    lin_grad = jnp.einsum(
        "sjcp,sjop->co", normed_all, mixed_pre, preferred_element_type=jnp.float32
    )[None]
    lin_grad = lax.psum(lin_grad, "dp")
    back_lin = sign_matrix(own_blade, "own")
    lin_sel = jnp.einsum(
        "ik,kco->ico", back_lin, lin_all, preferred_element_type=jnp.float32
    ).astype(jnp.bfloat16)
    from_lin = jnp.einsum("siop,ico->scp", pre_all, lin_sel, preferred_element_type=jnp.float32)[
        :, None
    ]
    input_grad = (cot_float + from_lin + from_spec) / normalizer
    spec_new, spec_first_new, spec_second_new = adamw(
        spec_weight, spec_first, spec_second, spec_grad
    )
    lin_new, lin_first_new, lin_second_new = adamw(lin_weight, lin_first, lin_second, lin_grad)
    return (
        output,
        input_grad,
        spec_new,
        spec_first_new,
        spec_second_new,
        lin_new,
        lin_first_new,
        lin_second_new,
    )


def solution(mesh):
    return jax.shard_map(
        body,
        mesh=mesh,
        in_specs=(
            P("dp", "blade", None, None),
            P("dp", "blade", None, None),
            P(),
            P("dp"),
            P("blade", "dp", None, None, None),
            P("blade", "dp", None, None, None),
            P("blade", "dp", None, None, None),
            P("blade", None, None),
            P("blade", None, None),
            P("blade", None, None),
        ),
        out_specs=(
            P("dp", "blade", None, None),
            P("dp", "blade", None, None),
            P("blade", "dp", None, None, None),
            P("blade", "dp", None, None, None),
            P("blade", "dp", None, None, None),
            P("blade", None, None),
            P("blade", None, None),
            P("blade", None, None),
        ),
        check_vma=False,
    )
```

profile of v0, /device:TPU:0, one launch (start us, length us, event | category | flops | bytes accessed | tf_op | source)
XLA Modules:
  0.0 696.8 jit_solution(13028528623821768969)
XLA Ops:
  10.8 16.9 %fusion.38 = (f32[4096,256]{1,0:T(8,128)S(1)}, f32[4096,256]{1,0:T(8,128)S(1)}) fusion(s32[256]{0:T(256)S(1)} %get-tuple-element.66, s32[4096]{0:T(1024)S(1)} %get-tuple-element.63, s32[256]{0:T(256)S(1)} %get-tuple-element.65, s32[4096]{0:T(1024)S(1)} %get-tuple-element.64), kind=kLoop, calls=%fused_computation.71 | loop fusion | flops 17825792 | bytes 8423424 | tf_op jit(solution)/shard_map/cos | solution.py:35
  36.3 31.1 %all-gather.14.cloned.1.call-done = bf16[8,192,512]{2,1,0:T(8,128)(2,1)} async-done(((bf16[8,48,512]{2,1,0:T(8,128)(2,1)}), bf16[8,192,512]{2,1,0:T(8,128)(2,1)}) %all-gather.14.cloned.1.call-update) | async-done | bytes 1572880 | tf_op jit(solution)/shard_map/all_gather | solution.py:92
  77.5 56.9 %all-gather.8.cloned.1.call-done = bf16[1,256,2,48,48]{4,3,1,2,0:T(8,128)(2,1)} async-done(((bf16[1,32,2,48,48]{4,3,1,2,0:T(8,128)(2,1)}), bf16[1,256,2,48,48]{4,3,1,2,0:T(8,128)(2,1)}) %all-gather.8.cloned.1.call-update) | async-done | bytes 2359312 | tf_op jit(solution)/shard_map/all_gather | solution.py:96
  144.5 6.7 copy.169
  155.7 8.6 %all_gather.21 = bf16[4,48,48]{2,1,0:T(8,128)(2,1)S(1)} all-gather(bf16[1,48,48]{2,1,0:T(8,128)(2,1)S(1)} %convert_element_type.106), channel_id=1, replica_groups=mesh['blade'=4,'dp'=8] {'blade'}, dimensions={0}, use_global_device_ids=true | all-gather | bytes 23040 | tf_op jit(solution)/shard_map/all_gather | solution.py:91
  164.7 33.1 %reduce-scatter.12.cloned.1.call-done = f32[8,1,48,2,256]{4,2,3,0,1:T(8,128)} async-done(((f32[8,4,48,2,256]{4,2,3,0,1:T(8,128)}), f32[8,1,48,2,256]{4,2,3,0,1:T(8,128)}) %reduce-scatter.12.cloned.1.call-update) | async-done | bytes 786448
  199.5 8.9 %fusion.66 = f32[8,48,4096]{2,1,0:T(8,128)} fusion(bf16[8,48,512]{2,1,0:T(8,128)(2,1)S(1)} %convert_element_type.103, f32[4096,256]{1,0:T(8,128)} %copy-done.10, f32[4096,256]{1,0:T(8,128)} %copy-done.9, f32[512]{0:T(512)S(1)} %maximum_multiply_fusion), kind=kOutput, calls=%fused_computation.97 | convolution fusion | flops 1616904192 | bytes 15075328 | tf_op jit(solution)/shard_map/sjcn,pn->sjcp/dot_general | solution.py:107
  208.4 113.6 %all-gather.10.cloned.1.call-done = bf16[8,4,48,4096]{3,2,0,1:T(8,128)(2,1)} async-done(((bf16[8,1,48,4096]{3,2,0,1:T(8,128)(2,1)}), bf16[8,4,48,4096]{3,2,0,1:T(8,128)(2,1)}) %all-gather.10.cloned.1.call-update) | async-done | bytes 12582928 | tf_op jit(solution)/shard_map/all_gather | solution.py:90
  322.0 21.2 %fusion.12 = (bf16[8,1,48,4096]{3,2,0,1:T(8,128)(2,1)S(1)}, f32[8,48,4096]{2,1,0:T(8,128)}, f32[8,48,4096]{2,1,0:T(8,128)}) fusion(bf16[8,1,48,4096]{3,2,1,0:T(8,128)(2,1)} %param.11, f32[8,48,4096]{2,1,0:T(8,128)} %fusion.66, bf16[8,4,48,4096]{3,2,0,1:T(8,128)(2,1)} %all-gather.10.cloned.1.call-done, bf16[4,48,48]{1,2,0:T(8,128)(2,1)S(1)} %copy.175), kind=kOutput, calls=%fused_computation.19 | convolution fusion | flops 720371712 | bytes 37767168 | tf_op jit(solution)/shard_map/sjcp,jco->sop/dot_general | solution.py:114
  343.2 7.1 %fusion.56 = bf16[8,48,512]{2,1,0:T(8,128)(2,1)} fusion(bf16[8,1,48,4096]{3,2,0,1:T(8,128)(2,1)S(1)} %get-tuple-element.54, f32[4096,256]{1,0:T(8,128)} %copy-done.10, f32[4096,256]{1,0:T(8,128)} %copy-done.9, f32[512]{0:T(512)S(1)} %maximum_multiply_fusion), kind=kOutput, calls=%fused_computation.92 | convolution fusion | flops 1617100800 | bytes 11929600 | tf_op jit(solution)/shard_map/sjcp,pn->sjcn/dot_general | solution.py:122
  350.8 30.7 %all-gather.16.cloned.1.call-done = bf16[8,192,512]{2,1,0:T(8,128)(2,1)} async-done(((bf16[8,48,512]{2,1,0:T(8,128)(2,1)}), bf16[8,192,512]{2,1,0:T(8,128)(2,1)}) %all-gather.16.cloned.1.call-update) | async-done | bytes 1572880 | tf_op jit(solution)/shard_map/all_gather | solution.py:127
  385.9 5.4 copy.184
  391.2 4.0 copy.183
  395.2 4.4 fusion.39
  407.8 5.5 copy.187
  425.9 12.8 %reshape.319 = bf16[256,4608]{1,0:T(8,128)(2,1)} reshape(bf16[256,2,48,48]{3,2,1,0:T(8,128)(2,1)} %copy.220) | data formatting | bytes 4718592
  440.6 8.3 %fusion.37 = bf16[8,1,48,4096]{3,2,1,0:T(8,128)(2,1)} fusion(f32[8,48,4096]{2,1,0:T(8,128)} %get-tuple-element.55, f32[8,48,4096]{2,1,0:T(8,128)} %get-tuple-element.62, f32[8]{0:T(128)S(1)} %select_reduce_fusion, bf16[8,1,48,4096]{3,2,1,0:T(8,128)(2,1)S(1)} %copy-done.12), kind=kLoop, calls=%fused_computation.69 | loop fusion | flops 9437184 | bytes 18874400
  450.4 8.3 %fusion.62 = f32[8,48,4096]{2,1,0:T(8,128)} fusion(bf16[8,48,512]{2,1,0:T(8,128)(2,1)S(1)} %convert_element_type.117, f32[4096,256]{1,0:T(8,128)} %copy-done.10, f32[4096,256]{1,0:T(8,128)} %copy-done.9), kind=kOutput, calls=%fused_computation.96 | convolution fusion | flops 1616904192 | bytes 15073280 | tf_op jit(solution)/shard_map/sjcn,pn->sjcp/dot_general | solution.py:161
  458.7 24.2 %reduce-scatter.10.cloned.1.call-done = bf16[32,4608]{1,0:T(8,128)(2,1)} async-done(((bf16[256,4608]{1,0:T(8,128)(2,1)}), bf16[32,4608]{1,0:T(8,128)(2,1)}) %reduce-scatter.10.cloned.1.call-update) | async-done | bytes 294928
  491.8 115.0 %all-gather.12.cloned.1.call-done = bf16[8,4,48,4096]{3,2,0,1:T(8,128)(2,1)} async-done(((bf16[8,1,48,4096]{3,2,0,1:T(8,128)(2,1)}), bf16[8,4,48,4096]{3,2,0,1:T(8,128)(2,1)}) %all-gather.12.cloned.1.call-update) | async-done | bytes 12582928 | tf_op jit(solution)/shard_map/all_gather | solution.py:126
  606.8 17.4 %convert_bitcast_fusion = bf16[8,4,48,4096]{3,1,2,0:T(4,128)(2,1)} fusion(bf16[8,4,48,4096]{3,2,0,1:T(8,128)(2,1)} %all-gather.12.cloned.1.call-done, s32[4]{0:T(128)S(1)} %multiply_subtract_fusion.3, s32[]{:T(128)S(6)} %axis_index.15), kind=kOutput, calls=%fused_computation.4 | convolution fusion | flops 56623168 | bytes 25165844 | tf_op jit(solution)/shard_map/ij,sicp->sjcp/dot_general | solution.py:132
  624.2 23.3 %fusion.59 = f32[1,48,48]{2,1,0:T(8,128)S(1)} fusion(bf16[8,4,48,4096]{3,2,0,1:T(8,128)(2,1)} %all-gather.10.cloned.1.call-done, bf16[8,4,48,4096]{3,1,2,0:T(4,128)(2,1)} %convert_bitcast_fusion), kind=kOutput, calls=%fused_computation.95 | convolution fusion | flops 603979776 | bytes 25175040 | tf_op jit(solution)/shard_map/sjcp,sjop->co/dot_general | solution.py:164
  647.5 28.5 %psum.7 = f32[1,48,48]{2,1,0:T(8,128)S(1)} all-reduce(f32[1,48,48]{2,1,0:T(8,128)S(1)} %fusion.59), channel_id=1, replica_groups=mesh['blade'=4,'dp'=8] {'dp'}, use_global_device_ids=true, to_apply=%region_4.5 | all-reduce | flops 2304 | bytes 18432 | tf_op jit(solution)/shard_map/psum | solution.py:167
  676.7 12.8 %fusion.16 = f32[8,1,48,4096]{3,2,1,0:T(8,128)} fusion(f32[8,48,4096]{2,1,0:T(8,128)} %fusion.62, bf16[8,4,48,4096]{3,2,0,1:T(8,128)(2,1)} %all-gather.12.cloned.1.call-done, bf16[8,1,48,4096]{3,2,1,0:T(8,128)(2,1)} %param.11, f32[8]{0:T(128)S(1)} %select_reduce_fusion, bf16[4,48,48]{2,0,1:T(4,128)(2,1)S(1)} %convolution_convert_fusion.1), kind=kOutput, calls=%fused_computation.23 | convolution fusion | flops 610271232 | bytes 28330016 | tf_op jit(solution)/shard_map/siop,ico->scp/dot_general | solution.py:172
  (106 shorter events, 77.2 us)
Async XLA Ops:
  7.2 60.3 %all-gather.14.cloned.1.call-start = ((), (), s32[]{:S(2)}) async-start(), calls=%async_computation.6 | async-start | bytes 1966080 | tf_op jit(solution)/shard_map/all_gather | solution.py:92
  10.8 16.9 %copy-start.11 = (bf16[8,1,48,4096]{3,2,0,1:T(8,128)(2,1)}, bf16[8,1,48,4096]{3,2,0,1:T(8,128)(2,1)S(1)}, u32[]{:S(2)}) copy-start(bf16[8,1,48,4096]{3,2,0,1:T(8,128)(2,1)S(1)} %fusion.30) | copy-start | bytes 9437188
  27.7 2.0 copy-start.9
  27.7 3.2 copy-start.10
  33.6 100.8 %all-gather.8.cloned.1.call-start = ((), (), s32[]{:S(2)}) async-start(), calls=%async_computation.3 | async-start | bytes 7077888 | tf_op jit(solution)/shard_map/all_gather | solution.py:96
  36.1 161.7 %reduce-scatter.12.cloned.1.call-start = ((), (), s32[]{:S(2)}) async-start(), calls=%async_computation.9 | async-start | bytes 3932160
  73.7 63.6 %copy-start.1 = (bf16[8,4,48,256]{2,0,1,3:T(8,128)(2,1)}, bf16[8,4,48,256]{2,0,1,3:T(8,128)(2,1)S(1)}, u32[]{:S(2)}) copy-start(bf16[8,4,48,256]{2,0,1,3:T(8,128)(2,1)S(1)} %copy.222) | copy-start | bytes 2359300
  134.4 3.7 copy-start
  155.0 167.0 %all-gather.10.cloned.1.call-start = ((), (), s32[]{:S(2)}) async-start(), calls=%async_computation.4 | async-start | bytes 15728640 | tf_op jit(solution)/shard_map/all_gather | solution.py:90
  155.6 225.9 %all-gather.16.cloned.1.call-start = ((), (), s32[]{:S(2)}) async-start(), calls=%async_computation.7 | async-start | bytes 1966080 | tf_op jit(solution)/shard_map/all_gather | solution.py:127
  343.2 7.1 %copy-start.14 = (bf16[8,1,48,4096]{3,2,0,1:T(8,128)(2,1)}, bf16[8,1,48,4096]{3,2,0,1:T(8,128)(2,1)S(1)}, u32[]{:S(2)}) copy-start(bf16[8,1,48,4096]{3,2,0,1:T(8,128)(2,1)S(1)} %get-tuple-element.54) | copy-start | bytes 9437188
  350.3 98.5 %reduce-scatter.14.cloned.1.call-start = ((), (), s32[]{:S(2)}) async-start(), calls=%async_computation.10 | async-start | bytes 1966080
  385.9 13.8 %slice-start = ((s8[6291456]{0:T(1024)(128)(4,1)}), s8[2097152]{0:T(1024)(128)(4,1)S(1)}, s32[]{:S(2)}) async-start(s8[6291456]{0:T(1024)(128)(4,1)} %bitcast.210), calls=%async_computation.11 | async-start | bytes 4194304
  395.2 4.4 slice-start.1
  395.2 4.4 copy-start.7
  401.4 1.8 copy-start.5
  407.8 5.7 copy-start.2
  413.4 69.6 %reduce-scatter.10.cloned.1.call-start = ((), (), s32[]{:S(2)}) async-start(), calls=%async_computation.8 | async-start | bytes 2654208
  413.6 2.8 copy-start.8
  438.7 1.9 copy-start.12
  438.7 168.1 %all-gather.12.cloned.1.call-start = ((), (), s32[]{:S(2)}) async-start(), calls=%async_computation.5 | async-start | bytes 15728640 | tf_op jit(solution)/shard_map/all_gather | solution.py:126
  450.4 34.3 %copy-start.13 = (f32[1,32,2,48,48]{4,3,2,1,0:T(8,128)S(1)}, f32[1,32,2,48,48]{4,3,2,1,0:T(8,128)}, u32[]{:S(2)}) copy-start(f32[1,32,2,48,48]{4,3,2,1,0:T(8,128)} %param.14) | copy-start | bytes 1769476
  624.2 51.8 %copy-start.16 = (f32[1,48,48]{2,1,0:T(8,128)S(1)}, f32[1,48,48]{2,1,0:T(8,128)}, u32[]{:S(2)}) copy-start(f32[1,48,48]{2,1,0:T(8,128)} %param.18) | copy-start | bytes 27652
  624.2 51.8 %copy-start.17 = (f32[1,48,48]{2,1,0:T(8,128)S(1)}, f32[1,48,48]{2,1,0:T(8,128)}, u32[]{:S(2)}) copy-start(f32[1,48,48]{2,1,0:T(8,128)} %param.19) | copy-start | bytes 27652
  (4 other events, 5.5 us)
Sparse Core Ops, SparseCore 0:
  33.7 33.6 all-gather.13
  69.6 64.7 all-gather.7
  155.1 42.6 reduce-scatter.11
  199.5 122.4 all-gather.9
  350.5 30.9 all-gather.15
  413.5 30.8 reduce-scatter.13
  446.7 36.1 reduce-scatter.9
  484.8 121.9 all-gather.11
where the time goes:
time: 706 us; the launch traced here: 697 us
  waiting for transfers between devices  406 us (58%)
  matrix products  128 us (18%)
  local copies, waits for them, and re-layouts  69 us (10%)
  other arithmetic  41 us (6%)
  blocking collectives  37.1 us (5%)
  between operations  15.1 us (2%)
    all_gather x1, waiting for transfers between devices, body(): lax.all_gather(grad_pre, 'blade', axis=1, tiled=True)  115 us
    all_gather x1, waiting for transfers between devices, body(): lax.all_gather(normed_low, 'blade', axis=1, tiled=True)  114 us
    unnamed x11, waiting for transfers between devices  58.4 us
    all_gather x1, waiting for transfers between devices, body(): block_in = lax.all_gather(spec_low, 'dp', axis=1, tiled=True)  56.9 us
    unnamed x49, local copies, waits for them, and re-layouts  38.6 us
    all_gather x1, waiting for transfers between devices, body(): lax.all_gather(own_modes, 'blade', axis=1, tiled=True)  31.1 us
    all_gather x1, waiting for transfers between devices, body(): lax.all_gather(grad_spec, 'blade', axis=1, tiled=True)  30.7 us
    psum x1, blocking collectives, body(): lin_grad = lax.psum(lin_grad, 'dp')  28.5 us
  transfers between devices with their start and end apart: 8, of which 7 were waited for; matrix products, arithmetic and copies ran while one was open for 11% of the time, Pallas kernels for 0%

commit v1 on v0

--- a/solution.py
+++ b/solution.py
@@ -93,7 +93,12 @@
     )
     modes_real = modes_all[..., :MODES]
     modes_imag = modes_all[..., MODES:]
-    block_in = lax.all_gather(spec_low, "dp", axis=1, tiled=True)
+    ring = [spec_low]
+    for hop in range(7):
+        ring.append(lax.ppermute(ring[-1], "dp", [(dev, (dev + 1) % 8) for dev in range(8)]))
+    block_in = jnp.roll(
+        jnp.concatenate(ring[::-1], axis=1), (lax.axis_index("dp") + 1) * ring[0].shape[1], axis=1
+    )
     w_real = block_in[0, :, 0]
     w_imag = block_in[0, :, 1]
     form = partial(jnp.einsum, "sjcm,mco->sjom", preferred_element_type=jnp.float32)

time: 706 us -> 777 us (1.10)
  waiting for transfers between devices: 406 us -> 445 us
  local copies, waits for them, and re-layouts: 69 us -> 90.6 us
  matrix products: 128 us -> 140 us
    ppermute x0 -> x7, waiting for transfers between devices: none -> 73.4 us  [body(): lax.ppermute(ring[-1], 'dp', [(dev, (dev + 1) % 8) for dev in range(8)])]
    all_gather x1, waiting for transfers between devices: 31.1 us -> 0.71 us  [body(): lax.all_gather(own_modes, 'blade', axis=1, tiled=True)]
    unnamed x49 -> x76, local copies, waits for them, and re-layouts: 38.6 us -> 59.1 us
  transfers between devices with their start and end apart: 8 -> 15, of which waited for: 7 -> 13; matrix products, arithmetic and copies ran while one was open for 11% -> 17% of each run, Pallas kernels for 0% -> 0%
where the time goes in v1:
time: 777 us; the launch traced here: 770 us
  waiting for transfers between devices  445 us (57%)
  matrix products  140 us (18%)
  local copies, waits for them, and re-layouts  90.6 us (12%)
  other arithmetic  40.8 us (5%)
  blocking collectives  37.1 us (5%)
  between operations  15.1 us (2%)
    all_gather x1, waiting for transfers between devices, body(): lax.all_gather(grad_pre, 'blade', axis=1, tiled=True)  115 us
    all_gather x1, waiting for transfers between devices, body(): lax.all_gather(normed_low, 'blade', axis=1, tiled=True)  114 us
    ppermute x7, waiting for transfers between devices, body(): lax.ppermute(ring[-1], 'dp', [(dev, (dev + 1) % 8) for dev in range(8)])  73.4 us
    unnamed x11, waiting for transfers between devices  59.6 us
    unnamed x76, local copies, waits for them, and re-layouts  59.1 us
    all_gather x1, waiting for transfers between devices, body(): block_in = lax.all_gather(spec_low, 'dp', axis=1, tiled=True)  52.6 us
    all_gather x1, waiting for transfers between devices, body(): lax.all_gather(grad_spec, 'blade', axis=1, tiled=True)  30.1 us
    psum x1, blocking collectives, body(): lin_grad = lax.psum(lin_grad, 'dp')  28.5 us
  transfers between devices with their start and end apart: 15, of which 13 were waited for; matrix products, arithmetic and copies ran while one was open for 17% of the time, Pallas kernels for 0%

profile of v1, /device:TPU:0, one launch (start us, length us, event | category | flops | bytes accessed | tf_op | source)
XLA Modules:
  0.0 770.3 jit_solution(10138904560858856376)
XLA Ops:
  9.3 13.7 %collective-permute-done = bf16[1,32,2,48,48]{4,3,1,2,0:T(8,128)(2,1)S(1)} collective-permute-done((bf16[1,32,2,48,48]{4,3,1,2,0:T(8,128)(2,1)S(1)}, bf16[1,32,2,48,48]{4,3,1,2,0:T(8,128)(2,1)S(1)}, u32[]{:S(2)}, u32[]{:S(2)}) %collective-permute-start) | collective-permute-done | bytes 294944 | tf_op jit(solution)/shard_map/ppermute | solution.py:98
  23.9 13.2 %collective-permute-done.1 = bf16[1,32,2,48,48]{4,3,1,2,0:T(8,128)(2,1)S(1)} collective-permute-done((bf16[1,32,2,48,48]{4,3,1,2,0:T(8,128)(2,1)S(1)}, bf16[1,32,2,48,48]{4,3,1,2,0:T(8,128)(2,1)S(1)}, u32[]{:S(2)}, u32[]{:S(2)}) %collective-permute-start.1) | collective-permute-done | bytes 294944 | tf_op jit(solution)/shard_map/ppermute | solution.py:98
  38.0 13.2 %collective-permute-done.2 = bf16[1,32,2,48,48]{4,3,1,2,0:T(8,128)(2,1)S(1)} collective-permute-done((bf16[1,32,2,48,48]{4,3,1,2,0:T(8,128)(2,1)S(1)}, bf16[1,32,2,48,48]{4,3,1,2,0:T(8,128)(2,1)S(1)}, u32[]{:S(2)}, u32[]{:S(2)}) %collective-permute-start.2) | collective-permute-done | bytes 294944 | tf_op jit(solution)/shard_map/ppermute | solution.py:98
  52.1 13.2 %collective-permute-done.3 = bf16[1,32,2,48,48]{4,3,1,2,0:T(8,128)(2,1)S(1)} collective-permute-done((bf16[1,32,2,48,48]{4,3,1,2,0:T(8,128)(2,1)S(1)}, bf16[1,32,2,48,48]{4,3,1,2,0:T(8,128)(2,1)S(1)}, u32[]{:S(2)}, u32[]{:S(2)}) %collective-permute-start.3) | collective-permute-done | bytes 294944 | tf_op jit(solution)/shard_map/ppermute | solution.py:98
  65.3 19.3 %fusion.46 = (f32[4096,256]{1,0:T(8,128)}, f32[4096,256]{1,0:T(8,128)}) fusion(s32[256]{0:T(256)S(1)} %get-tuple-element.66, s32[4096]{0:T(1024)S(1)} %get-tuple-element.63, s32[256]{0:T(256)S(1)} %get-tuple-element.65, s32[4096]{0:T(1024)S(1)} %get-tuple-element.64), kind=kLoop, calls=%fused_computation.81 | loop fusion | flops 17825792 | bytes 8423424 | tf_op jit(solution)/shard_map/cos | solution.py:35
  85.7 12.7 %collective-permute-done.5 = bf16[1,32,2,48,48]{4,3,1,2,0:T(8,128)(2,1)} collective-permute-done((bf16[1,32,2,48,48]{4,3,1,2,0:T(8,128)(2,1)}, bf16[1,32,2,48,48]{4,3,1,2,0:T(8,128)(2,1)}, u32[]{:S(2)}, u32[]{:S(2)}) %collective-permute-start.5) | collective-permute-done | bytes 294944 | tf_op jit(solution)/shard_map/ppermute | solution.py:98
  104.6 7.4 collective-permute-done.6
  162.0 7.1 copy.203
  175.1 8.6 %all_gather.19 = bf16[4,48,48]{2,1,0:T(8,128)(2,1)S(1)} all-gather(bf16[1,48,48]{2,1,0:T(8,128)(2,1)S(1)} %convert_element_type.106), channel_id=1, replica_groups=mesh['blade'=4,'dp'=8] {'blade'}, dimensions={0}, use_global_device_ids=true | all-gather | bytes 23040 | tf_op jit(solution)/shard_map/all_gather | solution.py:91
  184.1 34.4 %reduce-scatter.12.cloned.1.call-done = f32[8,1,48,2,256]{4,2,3,0,1:T(8,128)} async-done(((f32[8,4,48,2,256]{4,2,3,0,1:T(8,128)}), f32[8,1,48,2,256]{4,2,3,0,1:T(8,128)}) %reduce-scatter.12.cloned.1.call-update) | async-done | bytes 786448
  220.3 8.8 %fusion.70 = f32[8,48,4096]{2,1,0:T(8,128)} fusion(bf16[8,48,512]{2,1,0:T(8,128)(2,1)S(1)} %convert_element_type.103, f32[4096,256]{1,0:T(8,128)} %get-tuple-element.61, f32[4096,256]{1,0:T(8,128)} %get-tuple-element.60, f32[512]{0:T(512)S(1)} %maximum_multiply_fusion), kind=kOutput, calls=%fused_computation.103 | convolution fusion | flops 1616904192 | bytes 15075328 | tf_op jit(solution)/shard_map/sjcn,pn->sjcp/dot_general | solution.py:112
  229.1 113.8 %all-gather.8.cloned.1.call-done = bf16[8,4,48,4096]{3,2,0,1:T(8,128)(2,1)} async-done(((bf16[8,1,48,4096]{3,2,0,1:T(8,128)(2,1)}), bf16[8,4,48,4096]{3,2,0,1:T(8,128)(2,1)}) %all-gather.8.cloned.1.call-update) | async-done | bytes 12582928 | tf_op jit(solution)/shard_map/all_gather | solution.py:90
  342.9 22.7 %fusion.12 = (bf16[8,1,48,4096]{3,2,0,1:T(8,128)(2,1)}, f32[8,48,4096]{2,1,0:T(8,128)}, f32[8,48,4096]{2,1,0:T(8,128)}) fusion(bf16[8,1,48,4096]{3,2,1,0:T(8,128)(2,1)} %param.11, f32[8,48,4096]{2,1,0:T(8,128)} %fusion.70, bf16[8,4,48,4096]{3,2,0,1:T(8,128)(2,1)} %all-gather.8.cloned.1.call-done, bf16[4,48,48]{1,2,0:T(8,128)(2,1)S(1)} %copy.209), kind=kOutput, calls=%fused_computation.19 | convolution fusion | flops 720371712 | bytes 37767168 | tf_op jit(solution)/shard_map/sjcp,jco->sop/dot_general | solution.py:119
  373.5 30.1 %all-gather.16.cloned.1.call-done = bf16[8,192,512]{2,1,0:T(8,128)(2,1)} async-done(((bf16[8,48,512]{2,1,0:T(8,128)(2,1)}), bf16[8,192,512]{2,1,0:T(8,128)(2,1)}) %all-gather.16.cloned.1.call-update) | async-done | bytes 1572880 | tf_op jit(solution)/shard_map/all_gather | solution.py:132
  417.2 52.6 %all-gather.12.cloned.1.call-done = bf16[1,256,2,48,48]{4,3,1,2,0:T(8,128)(2,1)} async-done(((bf16[1,32,2,48,48]{4,3,1,2,0:T(8,128)(2,1)}), bf16[1,256,2,48,48]{4,3,1,2,0:T(8,128)(2,1)}) %all-gather.12.cloned.1.call-update) | async-done | bytes 2359312 | tf_op jit(solution)/shard_map/all_gather | solution.py:153
  501.0 12.9 %reshape.321 = bf16[256,4608]{1,0:T(8,128)(2,1)} reshape(bf16[256,2,48,48]{3,2,1,0:T(8,128)(2,1)} %copy.256) | data formatting | bytes 4718592
  515.0 8.2 %fusion.37 = bf16[8,1,48,4096]{3,2,1,0:T(8,128)(2,1)} fusion(f32[8,48,4096]{2,1,0:T(8,128)} %get-tuple-element.55, f32[8,48,4096]{2,1,0:T(8,128)} %get-tuple-element.62, f32[8]{0:T(128)S(1)} %select_reduce_fusion, bf16[8,1,48,4096]{3,2,1,0:T(8,128)(2,1)S(1)} %copy-done.11), kind=kLoop, calls=%fused_computation.71 | loop fusion | flops 9437184 | bytes 18874400
  524.9 8.3 %fusion.66 = f32[8,48,4096]{2,1,0:T(8,128)} fusion(bf16[8,48,512]{2,1,0:T(8,128)(2,1)S(1)} %convert_element_type.117, f32[4096,256]{1,0:T(8,128)} %get-tuple-element.61, f32[4096,256]{1,0:T(8,128)} %get-tuple-element.60), kind=kOutput, calls=%fused_computation.102 | convolution fusion | flops 1616904192 | bytes 15073280 | tf_op jit(solution)/shard_map/sjcn,pn->sjcp/dot_general | solution.py:166
  533.2 23.4 %reduce-scatter.10.cloned.1.call-done = bf16[32,4608]{1,0:T(8,128)(2,1)} async-done(((bf16[256,4608]{1,0:T(8,128)(2,1)}), bf16[32,4608]{1,0:T(8,128)(2,1)}) %reduce-scatter.10.cloned.1.call-update) | async-done | bytes 294928
  565.4 114.8 %all-gather.10.cloned.1.call-done = bf16[8,4,48,4096]{3,2,0,1:T(8,128)(2,1)} async-done(((bf16[8,1,48,4096]{3,2,0,1:T(8,128)(2,1)}), bf16[8,4,48,4096]{3,2,0,1:T(8,128)(2,1)}) %all-gather.10.cloned.1.call-update) | async-done | bytes 12582928 | tf_op jit(solution)/shard_map/all_gather | solution.py:131
  680.2 17.4 %convert_bitcast_fusion = bf16[8,4,48,4096]{3,1,2,0:T(4,128)(2,1)} fusion(bf16[8,4,48,4096]{3,2,0,1:T(8,128)(2,1)} %all-gather.10.cloned.1.call-done, s32[4]{0:T(128)S(1)} %multiply_subtract_fusion.3, s32[]{:T(128)S(6)} %axis_index.25), kind=kOutput, calls=%fused_computation.4 | convolution fusion | flops 56623168 | bytes 25165844 | tf_op jit(solution)/shard_map/ij,sicp->sjcp/dot_general | solution.py:137
  697.7 23.3 %fusion.63 = f32[1,48,48]{2,1,0:T(8,128)S(1)} fusion(bf16[8,4,48,4096]{3,2,0,1:T(8,128)(2,1)} %all-gather.8.cloned.1.call-done, bf16[8,4,48,4096]{3,1,2,0:T(4,128)(2,1)} %convert_bitcast_fusion), kind=kOutput, calls=%fused_computation.101 | convolution fusion | flops 603979776 | bytes 25175040 | tf_op jit(solution)/shard_map/sjcp,sjop->co/dot_general | solution.py:169
  720.9 28.5 %psum.7 = f32[1,48,48]{2,1,0:T(8,128)S(1)} all-reduce(f32[1,48,48]{2,1,0:T(8,128)S(1)} %fusion.63), channel_id=1, replica_groups=mesh['blade'=4,'dp'=8] {'dp'}, use_global_device_ids=true, to_apply=%region_4.5 | all-reduce | flops 2304 | bytes 18432 | tf_op jit(solution)/shard_map/psum | solution.py:172
  750.1 12.8 %fusion.16 = f32[8,1,48,4096]{3,2,1,0:T(8,128)} fusion(f32[8,48,4096]{2,1,0:T(8,128)} %fusion.66, bf16[8,4,48,4096]{3,2,0,1:T(8,128)(2,1)} %all-gather.10.cloned.1.call-done, bf16[8,1,48,4096]{3,2,1,0:T(8,128)(2,1)} %param.11, f32[8]{0:T(128)S(1)} %select_reduce_fusion, bf16[4,48,48]{2,0,1:T(4,128)(2,1)S(1)} %convolution_convert_fusion.1), kind=kOutput, calls=%fused_computation.23 | convolution fusion | flops 610271232 | bytes 28330016 | tf_op jit(solution)/shard_map/siop,ico->scp/dot_general | solution.py:177
  (147 shorter events, 134.6 us)
Async XLA Ops:
  7.2 77.4 %copy-start.24 = (f32[16]{0:T(128)S(1)}, f32[16]{0:T(128)}, u32[]{:S(2)}) copy-start(f32[16]{0:T(128)} %param.12) | copy-start | bytes 196
  7.2 77.4 %copy-start.25 = (s32[8]{0:T(128)S(1)}, s32[8]{0:T(128)}, u32[]{:S(2)}) copy-start(s32[8]{0:T(128)} %param.13) | copy-start | bytes 100
  7.2 130.1 %all-gather.14.cloned.1.call-start = ((), (), s32[]{:S(2)}) async-start(), calls=%async_computation.6 | async-start | bytes 1966080 | tf_op jit(solution)/shard_map/all_gather | solution.py:92
  8.7 76.1 %copy-start.20 = (bf16[1,32,2,48,48]{4,3,1,2,0:T(8,128)(2,1)}, bf16[1,32,2,48,48]{4,3,1,2,0:T(8,128)(2,1)S(1)}, u32[]{:S(2)}) copy-start(bf16[1,32,2,48,48]{4,3,1,2,0:T(8,128)(2,1)S(1)} %copy.290) | copy-start | bytes 884740
  8.8 76.1 %copy-start.10 = (bf16[8,1,48,4096]{3,2,1,0:T(8,128)(2,1)S(1)}, bf16[8,1,48,4096]{3,2,1,0:T(8,128)(2,1)}, u32[]{:S(2)}) copy-start(bf16[8,1,48,4096]{3,2,1,0:T(8,128)(2,1)} %param.10) | copy-start | bytes 9437188
  8.8 14.2 %collective-permute-start = (bf16[1,32,2,48,48]{4,3,1,2,0:T(8,128)(2,1)S(1)}, bf16[1,32,2,48,48]{4,3,1,2,0:T(8,128)(2,1)S(1)}, u32[]{:S(2)}, u32[]{:S(2)}) collective-permute-start(bf16[1,32,2,48,48]{4,3,1,2,0:T(8,128)(2,1)S(1)} %copy.290), channel_id=1, source_target_pairs={{0,1},{1,2},{2,3},{3,4},{4,5},{5,6},{6,7},{7,0},{8,9},{9,10},{10,1... | collective-permute-start | bytes 884744 | tf_op jit(solution)/shard_map/ppermute | solution.py:98
  23.9 13.2 %collective-permute-start.1 = (bf16[1,32,2,48,48]{4,3,1,2,0:T(8,128)(2,1)S(1)}, bf16[1,32,2,48,48]{4,3,1,2,0:T(8,128)(2,1)S(1)}, u32[]{:S(2)}, u32[]{:S(2)}) collective-permute-start(bf16[1,32,2,48,48]{4,3,1,2,0:T(8,128)(2,1)S(1)} %collective-permute-done), channel_id=1, source_target_pairs={{0,1},{1,2},{2,3},{3,4},{4,5},{5,6},{6,7},{7,0},{8,9},{9,10},{10,1... | collective-permute-start | bytes 884744 | tf_op jit(solution)/shard_map/ppermute | solution.py:98
  38.0 13.2 %collective-permute-start.2 = (bf16[1,32,2,48,48]{4,3,1,2,0:T(8,128)(2,1)S(1)}, bf16[1,32,2,48,48]{4,3,1,2,0:T(8,128)(2,1)S(1)}, u32[]{:S(2)}, u32[]{:S(2)}) collective-permute-start(bf16[1,32,2,48,48]{4,3,1,2,0:T(8,128)(2,1)S(1)} %collective-permute-done.1), channel_id=1, source_target_pairs={{0,1},{1,2},{2,3},{3,4},{4,5},{5,6},{6,7},{7,0},{8,9},{9,10},{10,1... | collective-permute-start | bytes 884744 | tf_op jit(solution)/shard_map/ppermute | solution.py:98
  52.1 13.2 %collective-permute-start.3 = (bf16[1,32,2,48,48]{4,3,1,2,0:T(8,128)(2,1)S(1)}, bf16[1,32,2,48,48]{4,3,1,2,0:T(8,128)(2,1)S(1)}, u32[]{:S(2)}, u32[]{:S(2)}) collective-permute-start(bf16[1,32,2,48,48]{4,3,1,2,0:T(8,128)(2,1)S(1)} %collective-permute-done.2), channel_id=1, source_target_pairs={{0,1},{1,2},{2,3},{3,4},{4,5},{5,6},{6,7},{7,0},{8,9},{9,10},{10,1... | collective-permute-start | bytes 884744 | tf_op jit(solution)/shard_map/ppermute | solution.py:98
  65.3 19.6 %copy-start.18 = (bf16[1,32,2,48,48]{4,3,1,2,0:T(8,128)(2,1)}, bf16[1,32,2,48,48]{4,3,1,2,0:T(8,128)(2,1)S(1)}, u32[]{:S(2)}) copy-start(bf16[1,32,2,48,48]{4,3,1,2,0:T(8,128)(2,1)S(1)} %collective-permute-done.3) | copy-start | bytes 884740
  65.3 19.5 %collective-permute-start.4 = (bf16[1,32,2,48,48]{4,3,1,2,0:T(8,128)(2,1)S(1)}, bf16[1,32,2,48,48]{4,3,1,2,0:T(8,128)(2,1)}, u32[]{:S(2)}, u32[]{:S(2)}) collective-permute-start(bf16[1,32,2,48,48]{4,3,1,2,0:T(8,128)(2,1)S(1)} %collective-permute-done.3), channel_id=1, source_target_pairs={{0,1},{1,2},{2,3},{3,4},{4,5},{5,6},{6,7},{7,0},{8,9},{9,10},{10,1... | collective-permute-start | bytes 884744 | tf_op jit(solution)/shard_map/ppermute | solution.py:98
  84.8 13.6 %collective-permute-start.5 = (bf16[1,32,2,48,48]{4,3,1,2,0:T(8,128)(2,1)}, bf16[1,32,2,48,48]{4,3,1,2,0:T(8,128)(2,1)}, u32[]{:S(2)}, u32[]{:S(2)}) collective-permute-start(bf16[1,32,2,48,48]{4,3,1,2,0:T(8,128)(2,1)} %collective-permute-done.4), channel_id=1, source_target_pairs={{0,1},{1,2},{2,3},{3,4},{4,5},{5,6},{6,7},{7,0},{8,9},{9,10},{10,1... | collective-permute-start | bytes 884744 | tf_op jit(solution)/shard_map/ppermute | solution.py:98
  98.4 13.5 %collective-permute-start.6 = (bf16[1,32,2,48,48]{4,3,1,2,0:T(8,128)(2,1)}, bf16[1,32,2,48,48]{4,3,1,2,0:T(8,128)(2,1)}, u32[]{:S(2)}, u32[]{:S(2)}) collective-permute-start(bf16[1,32,2,48,48]{4,3,1,2,0:T(8,128)(2,1)} %collective-permute-done.5), channel_id=1, source_target_pairs={{0,1},{1,2},{2,3},{3,4},{4,5},{5,6},{6,7},{7,0},{8,9},{9,10},{10,1... | collective-permute-start | bytes 884744 | tf_op jit(solution)/shard_map/ppermute | solution.py:98
  104.4 19.5 %copy-start.6 = (f32[1,32,2,48,48]{4,3,2,1,0:T(8,128)S(1)}, f32[1,32,2,48,48]{4,3,2,1,0:T(8,128)}, u32[]{:S(2)}) copy-start(f32[1,32,2,48,48]{4,3,2,1,0:T(8,128)} %param.14) | copy-start | bytes 1769476
  104.5 114.0 %reduce-scatter.12.cloned.1.call-start = ((), (), s32[]{:S(2)}) async-start(), calls=%async_computation.9 | async-start | bytes 3932160
  174.3 168.6 %all-gather.8.cloned.1.call-start = ((), (), s32[]{:S(2)}) async-start(), calls=%async_computation.3 | async-start | bytes 15728640 | tf_op jit(solution)/shard_map/all_gather | solution.py:90
  175.0 228.6 %all-gather.16.cloned.1.call-start = ((), (), s32[]{:S(2)}) async-start(), calls=%async_computation.7 | async-start | bytes 1966080 | tf_op jit(solution)/shard_map/all_gather | solution.py:132
  372.4 97.3 %all-gather.12.cloned.1.call-start = ((), (), s32[]{:S(2)}) async-start(), calls=%async_computation.5 | async-start | bytes 7077888 | tf_op jit(solution)/shard_map/all_gather | solution.py:153
  373.0 150.2 %reduce-scatter.14.cloned.1.call-start = ((), (), s32[]{:S(2)}) async-start(), calls=%async_computation.10 | async-start | bytes 1966080
  488.2 68.4 %reduce-scatter.10.cloned.1.call-start = ((), (), s32[]{:S(2)}) async-start(), calls=%async_computation.8 | async-start | bytes 2654208
  513.9 166.3 %all-gather.10.cloned.1.call-start = ((), (), s32[]{:S(2)}) async-start(), calls=%async_computation.4 | async-start | bytes 15728640 | tf_op jit(solution)/shard_map/all_gather | solution.py:131
  524.9 33.5 %copy-start.7 = (f32[1,32,2,48,48]{4,3,2,1,0:T(8,128)S(1)}, f32[1,32,2,48,48]{4,3,2,1,0:T(8,128)}, u32[]{:S(2)}) copy-start(f32[1,32,2,48,48]{4,3,2,1,0:T(8,128)} %param.14) | copy-start | bytes 1769476
  697.7 51.8 %copy-start.22 = (f32[1,48,48]{2,1,0:T(8,128)S(1)}, f32[1,48,48]{2,1,0:T(8,128)}, u32[]{:S(2)}) copy-start(f32[1,48,48]{2,1,0:T(8,128)} %param.18) | copy-start | bytes 27652
  697.7 51.8 %copy-start.23 = (f32[1,48,48]{2,1,0:T(8,128)S(1)}, f32[1,48,48]{2,1,0:T(8,128)}, u32[]{:S(2)}) copy-start(f32[1,48,48]{2,1,0:T(8,128)} %param.19) | copy-start | bytes 27652
  (17 other events, 118.3 us)
Sparse Core Ops, SparseCore 0:
  104.6 32.6 all-gather.13
  174.4 44.0 reduce-scatter.11
  220.3 122.4 all-gather.7
  372.6 30.9 all-gather.15
  405.0 64.7 all-gather.11
  488.4 29.6 reduce-scatter.13
  520.3 36.2 reduce-scatter.9
  558.4 121.7 all-gather.9
